TPU v7x, 256 devices: a whole 4x4x8 slice. The times are simulated.
256 devices in a mesh: dp: 16 (over z, core), mp: 16 (over y, x).
Axes of the slice: x: 4, y: 4, z: 8, core: 2. Of those that a mesh axis runs over, the one named last changes fastest.
Arguments:
- tokens: bfloat16 [49152, 8192], P('dp', 'mp'), may hold values from -6 to 6
- frozen_weight: bfloat16 [8192, 2048], P('mp', 'dp'), may hold values from -0.0625 to 0.0625
- adapter_down_weight: bfloat16 [8192, 4096], P(None, 'mp'), may hold values from -0.0625 to 0.0625
- adapter_up_weight: bfloat16 [2, 128, 16, 1024], P(None, 'mp'), may hold values from -1.5 to 1.5
- token_adapter_index: int32 [49152], P('dp'), may hold values from 0 to 127, as said below
Outputs:
- projected: bfloat16 [49152, 2048], P(('dp', 'mp'))
Inputs may be any that keep to these rules, and one draw needn't show every extreme that they name: `token_adapter_index`: A token's owner is its adapter id divided by 8, rounded down. Of the 192 tokens of each aligned block of rows (the rows of one device's output), at most 24 have the same owner; in each run of 16 such blocks that one dp index holds, one owner has exactly 24 tokens in every block.
All inputs are finite; a program needn't handle non-finite values.
Results may differ from a plain program's by a relative error of at most 0.0055.
Values may be sent and summed in bfloat16 or wider, within the bound.
A program may use at most 128 MiB of HBM per device.

v0:
```python
import jax
import jax.numpy as jnp
from jax import lax
from jax.sharding import PartitionSpec as P

ADAPTER_SCALE = 2.0


def local(tokens, frozen_weight, adapter_down_weight, adapter_up_weight, token_adapter_index):
    mp_count = lax.axis_size("mp")
    position = lax.axis_index("mp")
    group_rows, feature_cols = tokens.shape
    own_rows = group_rows // mp_count
    capacity = 2 * own_rows // mp_count
    hidden_width = adapter_down_weight.shape[0]
    present_adapters = adapter_up_weight.shape[1]
    rank_extent = adapter_up_weight.shape[2]
    key_value_span = adapter_up_weight.shape[3]
    both_width = 2 * key_value_span
    per_owner = mp_count * capacity
    slot_total = mp_count * per_owner
    owners_of = token_adapter_index // present_adapters
    local_adapter = token_adapter_index % present_adapters
    owner_hits = (owners_of[:, None] == jnp.arange(mp_count, dtype=jnp.int32)[None, :]).astype(
        jnp.int32
    )
    running = jnp.cumsum(owner_hits.reshape(mp_count, own_rows, mp_count), axis=1).reshape(
        group_rows, mp_count
    )
    order_in = jnp.sum(running * owner_hits, axis=1) - 1
    block_index = jnp.arange(group_rows, dtype=jnp.int32) // own_rows
    slot_index = owners_of * per_owner + block_index * capacity + order_in
    slot_token = (
        jnp.full((slot_total,), group_rows, jnp.int32)
        .at[slot_index]
        .set(jnp.arange(group_rows, dtype=jnp.int32))
    )
    slot_adapter = jnp.full((slot_total,), -1, jnp.int32).at[slot_index].set(local_adapter)
    padded = jnp.concatenate([tokens, jnp.zeros((1, feature_cols), tokens.dtype)], axis=0)
    outgoing = jnp.take(padded, slot_token, axis=0).reshape(
        mp_count, mp_count, capacity, feature_cols
    )
    labels = slot_adapter.reshape(mp_count, mp_count, capacity, 1)
    key_up_weight = adapter_up_weight[0].reshape(present_adapters * rank_extent, key_value_span)
    value_up_weight = adapter_up_weight[1].reshape(present_adapters * rank_extent, key_value_span)
    received = lax.all_to_all(outgoing, "mp", split_axis=0, concat_axis=3, tiled=True)
    tags = lax.all_to_all(labels, "mp", split_axis=0, concat_axis=3, tiled=True)
    items = received.shape[2]
    flat_tokens = received.reshape(-1, hidden_width)
    adapter_tag = tags[..., 0].reshape(-1)
    full_projection = jnp.dot(flat_tokens, adapter_down_weight, preferred_element_type=jnp.float32)
    selector = (
        adapter_tag[:, None] == jnp.arange(present_adapters, dtype=jnp.int32)[None, :]
    ).astype(jnp.float32)
    low_rows = (
        full_projection.reshape(-1, present_adapters, 2, rank_extent) * selector[:, :, None, None]
    ).astype(jnp.bfloat16)
    key_section = jnp.dot(
        low_rows[:, :, 0, :].reshape(-1, present_adapters * rank_extent),
        key_up_weight,
        preferred_element_type=jnp.float32,
    )
    value_section = jnp.dot(
        low_rows[:, :, 1, :].reshape(-1, present_adapters * rank_extent),
        value_up_weight,
        preferred_element_type=jnp.float32,
    )
    adapter_updates = (
        ADAPTER_SCALE * jnp.concatenate([key_section, value_section], axis=1)
    ).astype(jnp.bfloat16)
    adapter_updates = adapter_updates.reshape(1, mp_count, items, both_width)
    arrived = lax.all_to_all(adapter_updates, "mp", split_axis=1, concat_axis=0, tiled=True)
    weight_full = lax.all_gather(frozen_weight, "dp", axis=1, tiled=True)
    own_owner = lax.dynamic_slice_in_dim(owners_of, position * own_rows, own_rows)
    own_order = lax.dynamic_slice_in_dim(order_in, position * own_rows, own_rows)
    own_delta = arrived[own_owner, 0, own_order]
    base_rows = lax.psum_scatter(
        jnp.dot(tokens, weight_full, preferred_element_type=jnp.float32),
        "mp",
        scatter_dimension=0,
        tiled=True,
    )
    return (base_rows + own_delta.astype(jnp.float32)).astype(jnp.bfloat16)


def solution(mesh):
    placed = (P("dp", "mp"), P("mp", "dp"), P(None, "mp"), P(None, "mp", None, None), P("dp"))
    return jax.shard_map(
        local, mesh=mesh, in_specs=placed, out_specs=P(("dp", "mp"), None), check_vma=False
    )
```

profile of v0, /device:TPU:32, one launch (start us, length us, event | category | flops | bytes accessed | tf_op | source)
XLA Modules:
  0.0 337.2 jit_solution(10187303301574286426)
XLA Ops:
  6.5 0.7 all-gather.2.cloned.1.call-update
  7.3 45.3 %all-gather.2.cloned.1.call-done = bf16[512,2048]{1,0:T(8,128)(2,1)} async-done(((bf16[512,128]{1,0:T(8,128)(2,1)}), bf16[512,2048]{1,0:T(8,128)(2,1)}) %all-gather.2.cloned.1.call-update) | async-done | bytes 2097168 | tf_op jit(solution)/shard_map/all_gather | solution.py:73
  52.6 13.7 %fusion.36 = f32[3072,2048]{1,0:T(8,128)} fusion(bf16[3072,512]{1,0:T(8,128)(2,1)} %param.5, bf16[512,2048]{1,0:T(8,128)(2,1)} %all-gather.2.cloned.1.call-done), kind=kOutput, calls=%fused_computation.67 | convolution fusion | flops 6442450944 | bytes 30408704 | tf_op jit(solution)/shard_map/dot_general | solution.py:78
  66.3 0.7 copy-done.1
  67.2 9.1 %reduce-window.6 = s32[16,16,2,128]{3,1,2,0:T(8,128)S(1)} reduce-window(s32[16,16,2,128]{3,1,2,0:T(8,128)S(1)} %copy_bitcast_fusion, s32[]{:T(128)} %constant.65.clone.1), window={size=1x1x1x128 pad=0_0x0_0x0_0x127_0}, to_apply=%region_1.2 | reduce-window | flops 8323072 | bytes 524292 | tf_op jit(solution)/shard_map/reduce-window
  76.2 0.1 slice.37
  76.4 0.3 copy.22
  76.7 0.1 bitcast_bitcast_fusion
  77.1 11.8 %scatter_custom_fusion.1 = s32[6144]{0:T(1024)S(1)} fusion(s32[3072]{0:T(1024)S(1)} %get-tuple-element.10, s32[3072]{0:T(1024)S(1)} %get-tuple-element.9, s32[]{:T(128)} %constant.68.clone.1), kind=kCustom, calls=%fused_computation.46 | custom fusion | bytes 24580 | tf_op jit(solution)/shard_map/scatter | solution.py:38
  89.0 0.7 reshape.188
  89.7 6.8 %all-to-all-start.1 = ((s32[16,1,384]{2,1,0:T(1,128)}), s32[16,1,384]{2,1,0:T(1,128)S(1)}, u32[]{:S(2)}, u32[]{:S(2)}) async-start(s32[16,1,384]{2,1,0:T(1,128)} %reshape.188), calls=%async_computation.2 | async-start | bytes 49152 | tf_op jit(solution)/shard_map/all_to_all | solution.py:47
  96.6 2.2 concatenate.20
  98.8 11.8 %scatter_custom_fusion = s32[6144]{0:T(1024)S(1)} fusion(s32[3072]{0:T(1024)S(1)} %get-tuple-element.10, s32[3072]{0:T(1024)S(1)} %iota.26, s32[]{:T(128)} %constant.63.clone.1), kind=kCustom, calls=%fused_computation.49 | custom fusion | bytes 24580 | tf_op jit(solution)/shard_map/scatter | solution.py:36
  110.8 25.5 %gather_fusion = bf16[6144,512]{1,0:T(8,128)(2,1)} fusion(bf16[3073,512]{1,0:T(8,128)(2,1)S(1)} %concatenate.20, s32[6144]{0:T(1024)S(1)} %fusion.13), kind=kCustom, calls=%fused_computation | custom fusion | bytes 12607488 | tf_op jit(solution)/shard_map/jit(_take)/gather | solution.py:40
  136.3 6.9 %broadcast_select_fusion = bf16[16,16,24,512]{3,2,1,0:T(8,128)(2,1)} fusion(bf16[16,16,24,512]{3,2,1,0:T(8,128)(2,1)} %bitcast.74, pred[16,16,24]{2,1,0:T(8,128)(4,1)S(1)} %broadcast_in_dim.40), kind=kLoop, calls=%fused_computation.6 | loop fusion | flops 3145728 | bytes 12589056 | tf_op jit(solution)/shard_map/jit(_take)/select_n | solution.py:40
  143.1 7.1 %all-to-all-start = ((bf16[16,16,24,512]{3,2,1,0:T(8,128)(2,1)}), bf16[16,16,24,512]{3,2,1,0:T(8,128)(2,1)}, u32[]{:S(2)}, u32[]{:S(2)}) async-start(bf16[16,16,24,512]{3,2,1,0:T(8,128)(2,1)} %broadcast_select_fusion), calls=%async_computation.1 | async-start | bytes 12582912 | tf_op jit(solution)/shard_map/all_to_all | solution.py:46
  150.3 6.6 %copy.26 = bf16[8192,256]{0,1:T(8,128)(2,1)} copy(bf16[8192,256]{1,0:T(8,128)(2,1)} %param.7) | data formatting | bytes 8388608 | tf_op args[2]
  156.9 0.5 broadcast.140
  157.5 0.7 reduce.1
  158.4 107.1 %all-to-all-done = bf16[16,16,24,512]{3,2,1,0:T(8,128)(2,1)} async-done(((bf16[16,16,24,512]{3,2,1,0:T(8,128)(2,1)}), bf16[16,16,24,512]{3,2,1,0:T(8,128)(2,1)}, u32[]{:S(2)}, u32[]{:S(2)}) %all-to-all-start) | async-done | bytes 6291488 | tf_op jit(solution)/shard_map/all_to_all | solution.py:46
  265.5 10.0 %copy.25 = bf16[1,16,24,16,512]{4,3,2,1,0:T(8,128)(2,1)} copy(bf16[1,16,24,16,512]{4,2,1,3,0:T(8,128)(2,1)} %bitcast.4) | data formatting | bytes 12582912 | tf_op jit(solution)/shard_map/all_to_all | solution.py:46
  275.5 10.5 %reshape.180 = bf16[384,8192,1,1]{1,0,2,3:T(8,128)(2,1)} reshape(bf16[1,16,24,16,512]{4,3,2,1,0:T(8,128)(2,1)} %copy.25) | data formatting | bytes 12582912 | tf_op jit(solution)/shard_map/reshape | solution.py:49
  286.0 6.5 %fusion.7 = bf16[384,8,2,16]{0,3,2,1:T(8,128)(2,1)S(1)} fusion(bf16[8,2,16,8192]{3,2,1,0:T(8,128)(2,1)} %bitcast.75, bf16[384,8192,1,1]{1,0,2,3:T(8,128)(2,1)} %reshape.180, f32[384,8]{0,1:T(8,128)S(1)} %fusion.26), kind=kOutput, calls=%fused_computation.14 | convolution fusion | flops 1610809344 | bytes 10694656 | tf_op jit(solution)/shard_map/dot_general | solution.py:51
  292.6 0.7 reshape.133
  293.2 0.7 reshape.132
  293.9 0.4 convolution_bitcast_fusion
  294.3 0.4 convolution_bitcast_fusion.1
  294.8 1.5 fusion.3
  296.2 3.9 %all-to-all-start.2 = ((bf16[1,16,24,2048]{3,2,0,1:T(8,128)(2,1)}), bf16[1,16,24,2048]{3,2,0,1:T(8,128)(2,1)S(1)}, u32[]{:S(2)}, u32[]{:S(2)}) async-start(bf16[1,16,24,2048]{3,2,0,1:T(8,128)(2,1)} %fusion.3), calls=%async_computation.3 | async-start | bytes 3145728 | tf_op jit(solution)/shard_map/all_to_all | solution.py:72
  300.3 22.9 %all-to-all-done.2 = bf16[1,16,24,2048]{3,2,0,1:T(8,128)(2,1)S(1)} async-done(((bf16[1,16,24,2048]{3,2,0,1:T(8,128)(2,1)}), bf16[1,16,24,2048]{3,2,0,1:T(8,128)(2,1)S(1)}, u32[]{:S(2)}, u32[]{:S(2)}) %all-to-all-start.2) | async-done | bytes 1572896 | tf_op jit(solution)/shard_map/all_to_all | solution.py:72
  323.2 4.7 %gather_fusion.1 = bf16[192,2048]{1,0:T(8,128)(2,1)S(1)} fusion(bf16[16,1,24,2048]{3,2,1,0:T(8,128)(2,1)S(1)} %bitcast.73, s32[192]{0:T(256)S(1)} %fusion.31), kind=kCustom, calls=%fused_computation.1 | custom fusion | bytes 1575168 | tf_op jit(solution)/shard_map/gather | solution.py:76
  327.9 2.5 add_convert_fusion
  (33 shorter events, 1.1 us)
Async XLA Ops:
  6.5 46.0 %all-gather.2.cloned.1.call-start = ((), (), s32[]{:S(2)}) async-start(), calls=%async_computation.4 | async-start | bytes 2228224 | tf_op jit(solution)/shard_map/all_gather | solution.py:73
  7.3 320.6 %reduce-scatter.2.cloned.1.call-start = ((), (), s32[]{:S(2)}) async-start(), calls=%async_computation.5 | async-start | bytes 26738688 | tf_op jit(solution)/shard_map/reduce_scatter | solution.py:77
  66.3 0.7 copy-start.1
  89.7 53.4 %all-to-all-start.1 = ((s32[16,1,384]{2,1,0:T(1,128)}), s32[16,1,384]{2,1,0:T(1,128)S(1)}, u32[]{:S(2)}, u32[]{:S(2)}) async-start(s32[16,1,384]{2,1,0:T(1,128)} %reshape.188), calls=%async_computation.2 | async-start | bytes 49152 | tf_op jit(solution)/shard_map/all_to_all | solution.py:47
  143.1 122.3 %all-to-all-start = ((bf16[16,16,24,512]{3,2,1,0:T(8,128)(2,1)}), bf16[16,16,24,512]{3,2,1,0:T(8,128)(2,1)}, u32[]{:S(2)}, u32[]{:S(2)}) async-start(bf16[16,16,24,512]{3,2,1,0:T(8,128)(2,1)} %broadcast_select_fusion), calls=%async_computation.1 | async-start | bytes 12582912 | tf_op jit(solution)/shard_map/all_to_all | solution.py:46
  150.3 6.6 %copy-start = (bf16[2,8,16,1024]{3,2,1,0:T(8,128)(2,1)S(1)}, bf16[2,8,16,1024]{3,2,1,0:T(8,128)(2,1)}, u32[]{:S(2)}) copy-start(bf16[2,8,16,1024]{3,2,1,0:T(8,128)(2,1)} %param.8) | copy-start | bytes 1572868
  296.2 26.9 %all-to-all-start.2 = ((bf16[1,16,24,2048]{3,2,0,1:T(8,128)(2,1)}), bf16[1,16,24,2048]{3,2,0,1:T(8,128)(2,1)S(1)}, u32[]{:S(2)}, u32[]{:S(2)}) async-start(bf16[1,16,24,2048]{3,2,0,1:T(8,128)(2,1)} %fusion.3), calls=%async_computation.3 | async-start | bytes 3145728 | tf_op jit(solution)/shard_map/all_to_all | solution.py:72
Sparse Core Ops, SparseCore 0:
  9.1 43.4 all-gather.1
  66.4 230.8 reduce-scatter.1
where the time goes:
time: 338 us; the launch traced here: 337 us
  waiting for transfers between devices  176 us (52%)
  local copies, waits for them, and re-layouts  87.4 us (26%)
  other arithmetic  21.1 us (6%)
  matrix products  21 us (6%)
  starting transfers between devices  17.9 us (5%)
  between operations  13.7 us (4%)
    all_to_all x1, waiting for transfers between devices, local(): lax.all_to_all(outgoing, 'mp', split_axis=0, concat_axis=3, tiled=True)  107 us
    all_gather x1, waiting for transfers between devices, local(): weight_full = lax.all_gather(frozen_weight, 'dp', axis=1, tiled=True)  45.3 us
    gather x1, local copies, waits for them, and re-layouts, local(): jnp.take(padded, slot_token, axis=0)  25.5 us
    all_to_all x1, waiting for transfers between devices, local(): lax.all_to_all(adapter_updates, 'mp', split_axis=1, concat_axis=0, tiled=...  22.9 us
    dot_general x1, matrix products, local(): jnp.dot(tokens, weight_full, preferred_element_type=jnp.float32)  13.7 us
    scatter x1, local copies, waits for them, and re-layouts, local(): jnp.full((slot_total,), -1, jnp.int32).at[slot_index].set(local_adapter)  11.8 us
    scatter x1, local copies, waits for them, and re-layouts, local(): slot_token = jnp.full((slot_total,), group_rows, jnp.int32).at[slot_index...  11.8 us
    reshape x1, local copies, waits for them, and re-layouts, local(): flat_tokens = received.reshape(-1, hidden_width)  10.5 us
  transfers between devices with their start and end apart: 5, of which 3 were waited for; matrix products, arithmetic and copies ran while one was open for 33% of the time, Pallas kernels for 0%

commit v1 on v0

--- a/solution.py
+++ b/solution.py
@@ -70,7 +70,9 @@
     ).astype(jnp.bfloat16)
     adapter_updates = adapter_updates.reshape(1, mp_count, items, both_width)
     arrived = lax.all_to_all(adapter_updates, "mp", split_axis=1, concat_axis=0, tiled=True)
-    weight_full = lax.all_gather(frozen_weight, "dp", axis=1, tiled=True)
+    weight_full = jnp.concatenate(
+        lax.all_to_all(jnp.stack([frozen_weight] * lax.axis_size("dp")), "dp", 0, 0), axis=1
+    )
     own_owner = lax.dynamic_slice_in_dim(owners_of, position * own_rows, own_rows)
     own_order = lax.dynamic_slice_in_dim(order_in, position * own_rows, own_rows)
     own_delta = arrived[own_owner, 0, own_order]

time: 338 us -> 354 us (1.047); the launches traced: 337 us -> 348 us
  blocking collectives: 0 us -> 56.6 us
  waiting for transfers between devices: 176 us -> 131 us
    all_to_all x0 -> x1, blocking collectives: none -> 56.6 us  [local(): lax.all_to_all(jnp.stack([frozen_weight] * lax.axis_size('dp')), 'dp', 0, 0)]
    all_gather x1 -> x0, waiting for transfers between devices: 45.3 us -> none  [local(): weight_full = lax.all_gather(frozen_weight, 'dp', axis=1, tiled=True)]
    unnamed x8 -> x11, local copies, waits for them, and re-layouts: 8.14 us -> 9.22 us
  transfers between devices with their start and end apart: 5 -> 4, of which waited for: 3 -> 2; matrix products, arithmetic and copies ran while one was open for 33% -> 32% of each run, Pallas kernels for 0% -> 0%
where the time goes in v1:
time: 354 us; the launch traced here: 348 us
  waiting for transfers between devices  131 us (37%)
  local copies, waits for them, and re-layouts  88.1 us (25%)
  blocking collectives  56.6 us (16%)
  other arithmetic  21.1 us (6%)
  matrix products  19.2 us (5%)
  starting transfers between devices  18.2 us (5%)
  between operations  13.7 us (4%)
    all_to_all x1, waiting for transfers between devices, local(): lax.all_to_all(outgoing, 'mp', split_axis=0, concat_axis=3, tiled=True)  107 us
    all_to_all x1, blocking collectives, local(): lax.all_to_all(jnp.stack([frozen_weight] * lax.axis_size('dp')), 'dp', 0, 0)  56.6 us
    gather x1, local copies, waits for them, and re-layouts, local(): jnp.take(padded, slot_token, axis=0)  25.5 us
    all_to_all x1, waiting for transfers between devices, local(): lax.all_to_all(adapter_updates, 'mp', split_axis=1, concat_axis=0, tiled=...  23.5 us
    dot_general x1, matrix products, local(): jnp.dot(tokens, weight_full, preferred_element_type=jnp.float32)  11.9 us
    scatter x1, local copies, waits for them, and re-layouts, local(): jnp.full((slot_total,), -1, jnp.int32).at[slot_index].set(local_adapter)  11.8 us
    scatter x1, local copies, waits for them, and re-layouts, local(): slot_token = jnp.full((slot_total,), group_rows, jnp.int32).at[slot_index...  11.8 us
    reshape x1, local copies, waits for them, and re-layouts, local(): flat_tokens = received.reshape(-1, hidden_width)  10.5 us
  transfers between devices with their start and end apart: 4, of which 2 were waited for; matrix products, arithmetic and copies ran while one was open for 32% of the time, Pallas kernels for 0%

profile of v1, /device:TPU:32, one launch (start us, length us, event | category | flops | bytes accessed | tf_op | source)
XLA Modules:
  0.0 347.7 jit_solution(13641599443898458680)
XLA Ops:
  6.5 1.0 copy.22
  7.6 0.2 stack.2
  7.8 56.6 %all_to_all.50 = bf16[16,512,128]{1,2,0:T(8,128)(2,1)S(1)} all-to-all(bf16[16,512,128]{1,2,0:T(8,128)(2,1)S(1)} %stack.2), channel_id=1, replica_groups=mesh['dp'=16,'mp'=16] {'dp'}, dimensions={0} | all-to-all | bytes 4194304 | tf_op jit(solution)/shard_map/all_to_all | solution.py:74
  64.3 11.9 %fusion.36 = f32[3072,2048]{1,0:T(8,128)} fusion(bf16[3072,512]{1,0:T(8,128)(2,1)S(1)} %copy-done, bf16[512,2048]{0,1:T(8,128)(2,1)S(1)} %bitcast.79), kind=kOutput, calls=%fused_computation.67 | convolution fusion | flops 6442450944 | bytes 30408704 | tf_op jit(solution)/shard_map/dot_general | solution.py:80
  76.3 0.7 copy-done.2
  77.1 9.1 %reduce-window.6 = s32[16,16,2,128]{3,1,2,0:T(8,128)S(1)} reduce-window(s32[16,16,2,128]{3,1,2,0:T(8,128)S(1)} %copy_bitcast_fusion, s32[]{:T(128)} %constant.65.clone.1), window={size=1x1x1x128 pad=0_0x0_0x0_0x127_0}, to_apply=%region_1.2 | reduce-window | flops 8323072 | bytes 524292 | tf_op jit(solution)/shard_map/reduce-window
  86.4 0.3 copy.24
  86.7 0.1 bitcast_bitcast_fusion
  87.0 11.8 %scatter_custom_fusion.1 = s32[6144]{0:T(1024)S(1)} fusion(s32[3072]{0:T(1024)S(1)} %get-tuple-element.10, s32[3072]{0:T(1024)S(1)} %get-tuple-element.9, s32[]{:T(128)} %constant.68.clone.1), kind=kCustom, calls=%fused_computation.46 | custom fusion | bytes 24580 | tf_op jit(solution)/shard_map/scatter | solution.py:38
  99.0 0.7 reshape.198
  99.7 7.0 %all-to-all-start.2 = ((s32[16,1,384]{2,1,0:T(1,128)}), s32[16,1,384]{2,1,0:T(1,128)S(1)}, u32[]{:S(2)}, u32[]{:S(2)}) async-start(s32[16,1,384]{2,1,0:T(1,128)} %reshape.198), calls=%async_computation.3 | async-start | bytes 49152 | tf_op jit(solution)/shard_map/all_to_all | solution.py:47
  106.8 2.2 concatenate.20
  109.0 11.8 %scatter_custom_fusion = s32[6144]{0:T(1024)S(1)} fusion(s32[3072]{0:T(1024)S(1)} %get-tuple-element.10, s32[3072]{0:T(1024)S(1)} %iota.26, s32[]{:T(128)} %constant.63.clone.1), kind=kCustom, calls=%fused_computation.49 | custom fusion | bytes 24580 | tf_op jit(solution)/shard_map/scatter | solution.py:36
  120.9 25.5 %gather_fusion = bf16[6144,512]{1,0:T(8,128)(2,1)} fusion(bf16[3073,512]{1,0:T(8,128)(2,1)S(1)} %concatenate.20, s32[6144]{0:T(1024)S(1)} %fusion.13), kind=kCustom, calls=%fused_computation | custom fusion | bytes 12607488 | tf_op jit(solution)/shard_map/jit(_take)/gather | solution.py:40
  146.4 6.9 %broadcast_select_fusion = bf16[16,16,24,512]{3,2,1,0:T(8,128)(2,1)} fusion(bf16[16,16,24,512]{3,2,1,0:T(8,128)(2,1)} %bitcast.77, pred[16,16,24]{2,1,0:T(8,128)(4,1)S(1)} %broadcast_in_dim.40), kind=kLoop, calls=%fused_computation.6 | loop fusion | flops 3145728 | bytes 12589056 | tf_op jit(solution)/shard_map/jit(_take)/select_n | solution.py:40
  153.3 7.2 %all-to-all-start.1 = ((bf16[16,16,24,512]{3,2,1,0:T(8,128)(2,1)}), bf16[16,16,24,512]{3,2,1,0:T(8,128)(2,1)}, u32[]{:S(2)}, u32[]{:S(2)}) async-start(bf16[16,16,24,512]{3,2,1,0:T(8,128)(2,1)} %broadcast_select_fusion), calls=%async_computation.2 | async-start | bytes 12582912 | tf_op jit(solution)/shard_map/all_to_all | solution.py:46
  160.5 6.7 %copy.28 = bf16[8192,256]{0,1:T(8,128)(2,1)} copy(bf16[8192,256]{1,0:T(8,128)(2,1)} %param.7) | data formatting | bytes 8388608 | tf_op args[2]
  167.3 0.5 broadcast.142
  167.8 0.7 reduce.1
  168.7 107.3 %all-to-all-done.1 = bf16[16,16,24,512]{3,2,1,0:T(8,128)(2,1)} async-done(((bf16[16,16,24,512]{3,2,1,0:T(8,128)(2,1)}), bf16[16,16,24,512]{3,2,1,0:T(8,128)(2,1)}, u32[]{:S(2)}, u32[]{:S(2)}) %all-to-all-start.1) | async-done | bytes 6291488 | tf_op jit(solution)/shard_map/all_to_all | solution.py:46
  276.0 9.5 %copy.27 = bf16[1,16,24,16,512]{4,3,2,1,0:T(8,128)(2,1)} copy(bf16[1,16,24,16,512]{4,2,1,3,0:T(8,128)(2,1)} %bitcast.6) | data formatting | bytes 12582912 | tf_op jit(solution)/shard_map/all_to_all | solution.py:46
  285.5 10.5 %reshape.190 = bf16[384,8192,1,1]{1,0,2,3:T(8,128)(2,1)} reshape(bf16[1,16,24,16,512]{4,3,2,1,0:T(8,128)(2,1)} %copy.27) | data formatting | bytes 12582912 | tf_op jit(solution)/shard_map/reshape | solution.py:49
  296.0 6.5 %fusion.7 = bf16[384,8,2,16]{0,3,2,1:T(8,128)(2,1)S(1)} fusion(bf16[8,2,16,8192]{3,2,1,0:T(8,128)(2,1)} %bitcast.78, bf16[384,8192,1,1]{1,0,2,3:T(8,128)(2,1)} %reshape.190, f32[384,8]{0,1:T(8,128)S(1)} %fusion.26), kind=kOutput, calls=%fused_computation.14 | convolution fusion | flops 1610809344 | bytes 10694656 | tf_op jit(solution)/shard_map/dot_general | solution.py:51
  302.5 0.7 reshape.143
  303.2 0.7 reshape.142
  303.9 0.4 convolution_bitcast_fusion
  304.3 0.4 convolution_bitcast_fusion.1
  304.7 1.5 fusion.3
  306.2 3.9 %all-to-all-start.3 = ((bf16[1,16,24,2048]{3,2,0,1:T(8,128)(2,1)}), bf16[1,16,24,2048]{3,2,0,1:T(8,128)(2,1)S(1)}, u32[]{:S(2)}, u32[]{:S(2)}) async-start(bf16[1,16,24,2048]{3,2,0,1:T(8,128)(2,1)} %fusion.3), calls=%async_computation.4 | async-start | bytes 3145728 | tf_op jit(solution)/shard_map/all_to_all | solution.py:72
  310.2 23.5 %all-to-all-done.3 = bf16[1,16,24,2048]{3,2,0,1:T(8,128)(2,1)S(1)} async-done(((bf16[1,16,24,2048]{3,2,0,1:T(8,128)(2,1)}), bf16[1,16,24,2048]{3,2,0,1:T(8,128)(2,1)S(1)}, u32[]{:S(2)}, u32[]{:S(2)}) %all-to-all-start.3) | async-done | bytes 1572896 | tf_op jit(solution)/shard_map/all_to_all | solution.py:72
  333.7 4.7 %gather_fusion.1 = bf16[192,2048]{1,0:T(8,128)(2,1)S(1)} fusion(bf16[16,1,24,2048]{3,2,1,0:T(8,128)(2,1)S(1)} %bitcast.76, s32[192]{0:T(256)S(1)} %fusion.31), kind=kCustom, calls=%fused_computation.1 | custom fusion | bytes 1575168 | tf_op jit(solution)/shard_map/gather | solution.py:78
  338.4 2.5 add_convert_fusion
  (35 shorter events, 1.2 us)
Async XLA Ops:
  6.5 331.8 %reduce-scatter.2.cloned.1.call-start = ((), (), s32[]{:S(2)}) async-start(), calls=%async_computation.5 | async-start | bytes 26738688 | tf_op jit(solution)/shard_map/reduce_scatter | solution.py:79
  7.5 56.8 %copy-start = (bf16[3072,512]{1,0:T(8,128)(2,1)S(1)}, bf16[3072,512]{1,0:T(8,128)(2,1)}, u32[]{:S(2)}) copy-start(bf16[3072,512]{1,0:T(8,128)(2,1)} %param.5) | copy-start | bytes 9437188
  76.3 0.7 copy-start.2
  99.7 53.6 %all-to-all-start.2 = ((s32[16,1,384]{2,1,0:T(1,128)}), s32[16,1,384]{2,1,0:T(1,128)S(1)}, u32[]{:S(2)}, u32[]{:S(2)}) async-start(s32[16,1,384]{2,1,0:T(1,128)} %reshape.198), calls=%async_computation.3 | async-start | bytes 49152 | tf_op jit(solution)/shard_map/all_to_all | solution.py:47
  153.3 122.7 %all-to-all-start.1 = ((bf16[16,16,24,512]{3,2,1,0:T(8,128)(2,1)}), bf16[16,16,24,512]{3,2,1,0:T(8,128)(2,1)}, u32[]{:S(2)}, u32[]{:S(2)}) async-start(bf16[16,16,24,512]{3,2,1,0:T(8,128)(2,1)} %broadcast_select_fusion), calls=%async_computation.2 | async-start | bytes 12582912 | tf_op jit(solution)/shard_map/all_to_all | solution.py:46
  160.5 6.7 %copy-start.1 = (bf16[2,8,16,1024]{3,2,1,0:T(8,128)(2,1)S(1)}, bf16[2,8,16,1024]{3,2,1,0:T(8,128)(2,1)}, u32[]{:S(2)}) copy-start(bf16[2,8,16,1024]{3,2,1,0:T(8,128)(2,1)} %param.8) | copy-start | bytes 1572868
  306.2 27.5 %all-to-all-start.3 = ((bf16[1,16,24,2048]{3,2,0,1:T(8,128)(2,1)}), bf16[1,16,24,2048]{3,2,0,1:T(8,128)(2,1)S(1)}, u32[]{:S(2)}, u32[]{:S(2)}) async-start(bf16[1,16,24,2048]{3,2,0,1:T(8,128)(2,1)} %fusion.3), calls=%async_computation.4 | async-start | bytes 3145728 | tf_op jit(solution)/shard_map/all_to_all | solution.py:72
Sparse Core Ops, SparseCore 0:
  76.4 231.8 reduce-scatter.1
